TPU v7x, 256 devices: a whole 4x4x8 slice. The times are simulated.
256 devices in a mesh: sect: 64 (over z, y, core), tp: 4 (over x).
Axes of the slice: x: 4, y: 4, z: 8, core: 2. Of those that a mesh axis runs over, the one named last changes fastest.
Arguments:
- item_hidden: bfloat16 [4096, 4096], P('sect', 'tp'), may hold values from -40 to 40
- item_gain: bfloat16 [4096], P('tp'), may hold values from 0.25 to 1.75
- send_item: int32 [64, 64, 4], P('sect'), may hold values from -1 to 63, as said below
- pos_slot: int32 [256, 192], P('sect'), may hold values from 0 to 255, as said below
- hist_len: int32 [256], P('sect'), may hold values from 64 to 128, as said below
- user_gain: bfloat16 [4096], P('tp'), may hold values from 0.25 to 1.75
- query_weight: bfloat16 [4096, 4096], P('tp', 'sect'), may hold values from -0.09375 to 0.09375
Outputs:
- item_grad: float32 [4096, 4096], P('sect', 'tp')
- user_loss: float32 [256], P('sect')
Inputs may be any that keep to these rules, and one draw needn't show every extreme that they name: `send_item`: entry [o, r, s] names item o * 64 + value, owned by device o and sent to reader r, or is -1 for an empty slot. Within one (o, r) block the named items are distinct and the filled slots come first; at least half of the 4 slots (rounded down, and at least one) are filled. In every draw some reader gets 4 filled slots from every owner. `pos_slot`: entry [u, j] names a filled slot of the buffer of the device holding user u, in the order o * 4 + s; every filled slot is named by some candidate or some history position below that user's length. `hist_len`: every device's block of 4 users holds a user of length 128.
All inputs are finite; a program needn't handle non-finite values.
Results may differ from a plain program's by a relative error of at most 0.015.
Values may be sent and summed in bfloat16 or wider, within the bound.
A program may use at most 128 MiB of HBM per device.

v0:
```python
import jax
import jax.numpy as jnp
from jax import lax
from jax.sharding import PartitionSpec as P

D = 4096
HD = 128
CAND = 64
NORM_FLOOR = 1e-06
LOGIT_SOFTNESS = 20.0


def head_norm(values, head_count):
    shaped = values.reshape(values.shape[:-1] + (head_count, values.shape[-1] // head_count))
    return shaped * lax.rsqrt(jnp.mean(shaped * shaped, axis=-1, keepdims=True) + NORM_FLOOR)


def causal_mask(lengths, history_span):
    position = jnp.arange(history_span)
    allowed = (position[None, :] <= position[:, None])[None] & (
        position[None, None, :] < lengths[:, None, None]
    )
    return allowed.astype(jnp.float32)


def attend(query_rows, normed_rows, attend_mask):
    head_count = query_rows.shape[-1] // HD
    query_heads = head_norm(query_rows, head_count).astype(jnp.bfloat16)
    key_heads = head_norm(normed_rows, head_count).astype(jnp.bfloat16)
    value_heads = normed_rows.astype(jnp.bfloat16).reshape(query_heads.shape)
    scores = jnp.einsum(
        "uihd,ujhd->uhij", query_heads, key_heads, preferred_element_type=jnp.float32
    ) * HD ** (-0.5)
    weights = jnp.exp(scores) * attend_mask[:, None]
    weights = weights / jnp.sum(weights, axis=-1, keepdims=True)
    mixed_rows = jnp.einsum(
        "uhij,ujhd->uihd",
        weights.astype(jnp.bfloat16),
        value_heads,
        preferred_element_type=jnp.float32,
    )
    return mixed_rows.reshape(query_rows.shape)


def score_parts(mixed_rows, history_rows, cand_rows):
    outputs = history_rows + mixed_rows
    follow = jnp.concatenate([history_rows[:, 1:], jnp.zeros_like(history_rows[:, :1])], axis=1)
    own_squares = jnp.sum(outputs * outputs, axis=-1)
    positive_dot_products = jnp.sum(outputs * follow, axis=-1)
    negative_dot_products = jnp.einsum(
        "uif,ucf->uic", outputs, cand_rows, precision=lax.Precision.HIGHEST
    )
    return (own_squares, positive_dot_products, negative_dot_products)


def user_losses(
    own_squares,
    positive_dot_products,
    negative_dot_products,
    next_item_square_sums,
    candidate_square_sums,
    lengths,
):
    reciprocal_norm = lax.rsqrt(own_squares + NORM_FLOOR)
    positive_target_logit = (
        LOGIT_SOFTNESS
        * positive_dot_products
        * reciprocal_norm
        * lax.rsqrt(next_item_square_sums + NORM_FLOOR)
    )
    negative_score_logits = (
        LOGIT_SOFTNESS
        * negative_dot_products
        * reciprocal_norm[..., None]
        * lax.rsqrt(candidate_square_sums + NORM_FLOOR)[:, None, :]
    )
    partition = jnp.exp(positive_target_logit) + jnp.sum(jnp.exp(negative_score_logits), axis=-1)
    terms = jnp.log(partition) - positive_target_logit
    position = jnp.arange(own_squares.shape[1])
    allowed = position[None, :] < lengths[:, None] - 1
    return jnp.sum(jnp.where(allowed, terms, 0.0), axis=-1) / (lengths - 1).astype(jnp.float32)


def slot_norm(slot_rows, slot_squares, gain_row):
    return slot_rows * lax.rsqrt(slot_squares / D + NORM_FLOOR)[:, None] * gain_row


def segment_rows(values, places, count):
    return jax.ops.segment_sum(
        values.reshape((-1,) + values.shape[2:]), places.reshape(-1), num_segments=count
    )


def local(item_hidden, item_gain, send_item, pos_slot, hist_len, user_gain, query_weight):
    hidden = item_hidden.astype(jnp.float32)
    item_squares = lax.psum(jnp.sum(hidden * hidden, axis=1), "tp")
    embedded = (
        hidden * lax.rsqrt(item_squares / D + NORM_FLOOR)[:, None] * item_gain.astype(jnp.float32)
    ).astype(jnp.bfloat16)
    send_slots = send_item[0]
    vacant = send_slots < 0
    picked = jnp.take(embedded, jnp.where(vacant, 0, send_slots), axis=0)
    outgoing = jnp.where(vacant[..., None], jnp.zeros((), jnp.bfloat16), picked)
    arrived = lax.all_to_all(outgoing, "sect", split_axis=0, concat_axis=0, tiled=True)
    feature_count = arrived.shape[-1]
    slot_rows = arrived.reshape(-1, feature_count).astype(jnp.float32)
    slot_count = slot_rows.shape[0]
    slot_squares = lax.psum(jnp.sum(slot_rows * slot_rows, axis=1), "tp")
    gain_row = user_gain.astype(jnp.float32)

    def norm_only(rows_in, squares_in):
        return slot_norm(rows_in, squares_in, gain_row)

    normed_slots, norm_back = jax.vjp(norm_only, slot_rows, slot_squares)
    normed_low = normed_slots.astype(jnp.bfloat16)
    partial_query = jnp.dot(
        normed_low,
        lax.all_gather(query_weight, "sect", axis=1, tiled=True),
        preferred_element_type=jnp.float32,
    )
    query_slots = lax.psum_scatter(
        partial_query.astype(jnp.bfloat16), "tp", scatter_dimension=1, tiled=True
    ).astype(jnp.float32)
    history_span = pos_slot.shape[1] - CAND
    hist_places = pos_slot[:, :history_span]
    cand_places = pos_slot[:, history_span:]
    follow_places = jnp.concatenate([hist_places[:, 1:], hist_places[:, :1]], axis=1)
    history_rows = slot_rows[hist_places]
    cand_rows = slot_rows[cand_places]
    normed_rows = normed_low[hist_places].astype(jnp.float32)
    query_rows = query_slots[hist_places]
    attend_mask = causal_mask(hist_len, history_span)

    def attend_only(query_in, normed_in):
        return attend(query_in, normed_in, attend_mask)

    mixed_rows, attend_back = jax.vjp(attend_only, query_rows, normed_rows)
    partial_stats, parts_back = jax.vjp(score_parts, mixed_rows, history_rows, cand_rows)
    own_squares, positive_dot_products, negative_dot_products = (
        lax.psum(partial_stats[0].astype(jnp.bfloat16), "tp").astype(jnp.float32),
        lax.psum(partial_stats[1].astype(jnp.bfloat16), "tp").astype(jnp.float32),
        lax.psum(partial_stats[2].astype(jnp.bfloat16), "tp").astype(jnp.float32),
    )
    next_item_square_sums = slot_squares[follow_places]
    candidate_square_sums = slot_squares[cand_places]

    def loss_only(own_in, hit_in, neg_in, follow_in, cand_in):
        return user_losses(own_in, hit_in, neg_in, follow_in, cand_in, hist_len)

    losses, loss_back = jax.vjp(
        loss_only,
        own_squares,
        positive_dot_products,
        negative_dot_products,
        next_item_square_sums,
        candidate_square_sums,
    )
    grad_own, grad_hit, grad_neg, grad_follow, grad_cand = loss_back(
        jnp.full(losses.shape, float(D), jnp.float32)
    )
    grad_mixed, grad_history, grad_cands = parts_back((grad_own, grad_hit, grad_neg))
    grad_query, grad_normed = attend_back(grad_mixed)
    grad_slots = segment_rows(grad_history, hist_places, slot_count) + segment_rows(
        grad_cands, cand_places, slot_count
    )
    grad_squares = segment_rows(grad_follow, follow_places, slot_count) + segment_rows(
        grad_cand, cand_places, slot_count
    )
    grad_norm_slots = segment_rows(grad_normed, hist_places, slot_count)
    grad_query_slots = segment_rows(grad_query, hist_places, slot_count)
    every_query = lax.all_gather(grad_query_slots.astype(jnp.bfloat16), "tp", axis=1, tiled=True)
    grad_from_query = lax.dot_general(
        every_query,
        lax.all_gather(query_weight, "sect", axis=1, tiled=True),
        (((1,), (1,)), ((), ())),
        preferred_element_type=jnp.float32,
    )
    grad_norm_slots = grad_norm_slots + grad_from_query
    back_rows, back_squares = norm_back(grad_norm_slots)
    back_squares = lax.psum(back_squares, "tp")
    grad_slots = grad_slots + back_rows + 2.0 * slot_rows * (grad_squares + back_squares)[:, None]
    returned = lax.all_to_all(
        grad_slots.reshape(arrived.shape).astype(jnp.bfloat16),
        "sect",
        split_axis=0,
        concat_axis=0,
        tiled=True,
    ).astype(jnp.float32)
    item_count = embedded.shape[0]
    targets = jnp.where(vacant, item_count, send_slots).reshape(-1)
    item_grad = jax.ops.segment_sum(
        returned.reshape(-1, feature_count), targets, num_segments=item_count + 1
    )[:item_count]
    return (item_grad, losses)


def solution(mesh):
    placed = (
        P("sect", "tp"),
        P("tp"),
        P("sect", None, None),
        P("sect", None),
        P("sect"),
        P("tp"),
        P("tp", "sect"),
    )
    return jax.shard_map(
        local, mesh=mesh, in_specs=placed, out_specs=(P("sect", "tp"), P("sect")), check_vma=False
    )
```

profile of v0, /device:TPU:1, one launch (start us, length us, event | category | flops | bytes accessed | tf_op | source)
XLA Modules:
  0.0 333.5 jit_solution(12200618832667628850)
XLA Ops:
  7.9 0.7 bitcast_compare_fusion
  10.4 1.0 fusion.29
  11.4 9.3 %psum.42 = f32[64]{0:T(128)S(1)} all-reduce(f32[64]{0:T(128)S(1)} %fusion.29), channel_id=1, replica_groups=mesh['sect'=64,'tp'=4] {'tp'}, use_global_device_ids=true, to_apply=%region_1.0 | all-reduce | flops 64 | bytes 512 | tf_op jit(solution)/shard_map/psum | solution.py:96
  20.7 1.0 fusion.31
  21.7 1.2 gather_fusion
  23.1 1.3 select_select_fusion
  24.4 14.3 %all-to-all-start = ((bf16[64,4,1024]{2,1,0:T(4,128)(2,1)}), bf16[64,4,1024]{2,1,0:T(4,128)(2,1)S(1)}, u32[]{:S(2)}, u32[]{:S(2)}) async-start(bf16[64,4,1024]{2,1,0:T(4,128)(2,1)} %select_select_fusion), calls=%async_computation | async-start | bytes 1048576 | tf_op jit(solution)/shard_map/all_to_all | solution.py:104
  38.9 19.4 %all-to-all-done = bf16[64,4,1024]{2,1,0:T(4,128)(2,1)S(1)} async-done(((bf16[64,4,1024]{2,1,0:T(4,128)(2,1)}), bf16[64,4,1024]{2,1,0:T(4,128)(2,1)S(1)}, u32[]{:S(2)}, u32[]{:S(2)}) %all-to-all-start) | async-done | bytes 524320 | tf_op jit(solution)/shard_map/all_to_all | solution.py:104
  58.9 6.0 %psum.43 = f32[256]{0:T(256)S(1)} all-reduce(f32[256]{0:T(256)S(1)} %reduce_sum.141), channel_id=1, replica_groups=mesh['sect'=64,'tp'=4] {'tp'}, use_global_device_ids=true, to_apply=%region_3.4 | all-reduce | flops 256 | bytes 2048 | tf_op jit(solution)/shard_map/psum | solution.py:108
  65.1 34.8 %all-gather.3.cloned.1.call-done = bf16[1024,4096]{0,1:T(8,128)(2,1)} async-done(((bf16[1024,64]{0,1:T(8,128)(2,1)}), bf16[1024,4096]{0,1:T(8,128)(2,1)}) %all-gather.3.cloned.1.call-update) | async-done | bytes 8388624 | tf_op jit(solution)/shard_map/all_gather | solution.py:118
  99.9 7.2 %convolution_convert_fusion = bf16[256,4096]{1,0:T(8,128)(2,1)} fusion(bf16[256,1024]{1,0:T(8,128)(2,1)S(1)} %multiply_convert_fusion.1, bf16[1024,4096]{0,1:T(8,128)(2,1)} %all-gather.3.cloned.1.call-done), kind=kOutput, calls=%fused_computation.14 | convolution fusion | flops 2148532224 | bytes 11010048 | tf_op jit(solution)/shard_map/dot_general | solution.py:116
  110.8 1.2 gather_fusion.5
  111.9 1.9 gather_fusion.6
  113.9 2.8 gather_fusion.2
  116.7 2.5 copy.131
  119.2 2.4 copy.110
  121.6 2.7 gather_fusion.1
  124.3 3.4 %copy.133 = f32[64,8,8,128]{3,2,1,0:T(8,128)} copy(f32[64,8,8,128]{3,1,2,0:T(8,128)} %bitcast.107) | data formatting | bytes 4194304
  127.6 3.1 copy.113
  130.8 1.6 slice.40
  132.5 3.5 %gather_fusion.4 = f32[512]{0:T(512)S(1)} fusion(f32[256]{0:T(256)S(1)} %psum.43, s32[1024]{0:T(1024)S(1)} %pad_clamp_fusion.1), kind=kCustom, calls=%fused_computation.4 | custom fusion | bytes 6144 | tf_op jit(solution)/shard_map/gather | solution.py:144
  136.2 1.1 convert_element_type.125
  137.4 2.7 gather_fusion.3
  140.1 2.1 copy.132
  142.1 1.4 multiply_reduce_fusion.1
  143.5 1.0 copy.105
  144.6 1.9 copy.106
  146.6 2.8 fusion.20
  150.1 0.8 fusion.18
  150.9 1.9 copy.112
  152.8 3.2 multiply_reduce_fusion
  156.0 2.0 convolution_convert_fusion.5
  158.1 8.6 %all-reduce.2 = (bf16[4,128]{1,0:T(4,128)(2,1)S(1)}, bf16[4,128]{1,0:T(4,128)(2,1)S(1)}) all-reduce(bf16[4,128]{1,0:T(4,128)(2,1)S(1)} %get-tuple-element.27, bf16[4,128]{1,0:T(4,128)(2,1)S(1)} %get-tuple-element.10), channel_id=1, replica_groups=mesh['sect'=64,'tp'=4] {'tp'}, use_global_device_ids=true, to_apply=%region_11.12 | all-reduce | flops 1024 | bytes 4096 | tf_op jit(solution)/shard_map/psum | solution.py:140
  167.3 34.6 %all-reduce.5.cloned.1.call-done = bf16[4,128,64]{1,2,0:T(8,128)(2,1)} async-done(((bf16[4,128,64]{1,2,0:T(8,128)(2,1)}), bf16[4,128,64]{1,2,0:T(8,128)(2,1)}) %all-reduce.5.cloned.1.call-update) | async-done | bytes 65552 | tf_op jit(solution)/shard_map/psum | solution.py:142
  201.9 1.0 fusion.38
  202.8 1.3 fusion.64
  205.0 0.8 fusion.40
  205.9 3.5 %pad_add_fusion = (f32[4,128,1024]{2,1,0:T(8,128)}, bf16[4,128,1024]{2,1,0:T(8,128)(2,1)}) fusion(f32[4,127,1024]{2,1,0:T(8,128)S(1)} %slice_multiply_fusion, f32[4,128,1024]{2,1,0:T(8,128)S(1)} %get-tuple-element.11, f32[4,128]{1,0:T(4,128)S(1)} %multiply_multiply_fusion.5, f32[4,127,1024]{2,1,0:T(8,128)S(1)} %copy-done.3, ...), kind=kOutput, calls=%fused_computation.48 | convolution fusion | flops 406552576 | bytes 10005504 | tf_op jit(solution)/shard_map/transpose(jvp(uif,ucf->uic))/dot_general | solution.py:50
  209.3 2.3 copy.130
  211.6 3.2 fusion.5
  215.4 1.1 fusion.16
  216.6 1.9 add_add_fusion.1
  218.5 2.9 copy.120
  221.4 7.5 %scatter_custom_fusion.2 = f32[256,1024]{1,0:T(8,128)} fusion(s32[512]{0:T(512)} %get-tuple-element.20, f32[64,8,8,128]{3,2,1,0:T(8,128)} %bitcast.114, f32[]{:T(128)} %constant.17.clone.1), kind=kCustom, calls=%fused_computation.37 | custom fusion | flops 524288 | bytes 3146240 | tf_op jit(solution)/shard_map/scatter-add | solution.py:89
  228.9 2.1 convert_element_type.143
  231.2 4.3 %fusion.9 = (f32[4,128,8]{1,2,0:T(8,128)S(1)}, bf16[4,8,128,128]{2,3,1,0:T(8,128)(2,1)S(1)}) fusion(bf16[4,128,8,128]{1,3,2,0:T(8,128)(2,1)} %copy.110, f32[4,128,8,128]{1,3,2,0:T(8,128)} %copy-done.1, f32[4,128,8]{1,2,0:T(8,128)S(1)} %get-tuple-element.37, bf16[4,8,128,128]{2,3,1,0:T(8,128)(2,1)} %copy-done.17, f32[4,8,128,128]{2,3,1,0:T(8,128)} %copy-done.9, ...), kind=kOutput, calls=%fused_computation.33 | convolution fusion | flops 141553664 | bytes 7667712 | tf_op jit(solution)/shard_map/transpose(jvp(uihd,ujhd->uhij))/dot_general | solution.py:31
  235.5 2.4 fusion.6
  237.9 3.0 copy.123
  241.0 2.3 scatter_custom_fusion.5
  243.3 2.3 fusion.43
  245.6 4.4 %scatter_custom_fusion.1 = f32[256,1024]{1,0:T(8,128)} fusion(s32[256]{0:T(256)S(1)} %reshape.374, f32[256,1024]{1,0:T(8,128)} %bitcast.124, f32[]{:T(128)} %constant.17.clone.1), kind=kCustom, calls=%fused_computation.68 | custom fusion | flops 262144 | bytes 1049088 | tf_op jit(solution)/shard_map/scatter-add | solution.py:89
  250.0 6.8 %scatter_custom_fusion = f32[256,1024]{1,0:T(8,128)} fusion(s32[512]{0:T(512)} %get-tuple-element.20, f32[512,1024]{1,0:T(8,128)} %bitcast.123, f32[]{:T(128)} %constant.17.clone.1), kind=kCustom, calls=%fused_computation.70 | custom fusion | flops 524288 | bytes 1049088 | tf_op jit(solution)/shard_map/scatter-add | solution.py:89
  256.8 4.2 %scatter_custom_fusion.4 = f32[256]{0:T(256)S(1)} fusion(s32[512]{0:T(512)S(1)} %add_bitcast_fusion, f32[512]{0:T(512)} %get-tuple-element.6, f32[]{:T(128)} %constant.17.clone.1), kind=kCustom, calls=%fused_computation.158 | custom fusion | flops 512 | bytes 1536 | tf_op jit(solution)/shard_map/scatter-add | solution.py:89
  261.1 5.7 %all-gather.5.cloned.1.call-done = bf16[256,4096]{1,0:T(8,128)(2,1)} async-done(((bf16[256,1024]{1,0:T(8,128)(2,1)}), bf16[256,4096]{1,0:T(8,128)(2,1)}) %all-gather.5.cloned.1.call-update) | async-done | bytes 2097168 | tf_op jit(solution)/shard_map/all_gather | solution.py:171
  266.8 7.4 %fusion.78 = f32[256,1024]{1,0:T(8,128)} fusion(bf16[256,4096]{1,0:T(8,128)(2,1)} %all-gather.5.cloned.1.call-done, bf16[1024,4096]{0,1:T(8,128)(2,1)} %all-gather.3.cloned.1.call-done), kind=kOutput, calls=%fused_computation.172 | convolution fusion | flops 2147483648 | bytes 11534336 | tf_op jit(solution)/shard_map/dot_general | solution.py:172
  274.2 7.4 %scatter_custom_fusion.3 = f32[256,1024]{1,0:T(8,128)} fusion(f32[256,1024]{1,0:T(8,128)} %fusion.78, s32[512]{0:T(512)} %get-tuple-element.20, f32[64,8,8,128]{3,2,1,0:T(8,128)S(1)} %bitcast.113), kind=kCustom, calls=%fused_computation.34 | custom fusion | flops 524288 | bytes 3145728 | tf_op jit(solution)/shard_map/scatter-add | solution.py:89
  281.6 1.5 multiply_reduce_fusion.2
  283.1 6.6 %psum.47 = f32[256]{0:T(256)S(1)} all-reduce(f32[256]{0:T(256)S(1)} %multiply_multiply_fusion.7), channel_id=1, replica_groups=mesh['sect'=64,'tp'=4] {'tp'}, use_global_device_ids=true, to_apply=%region_26.27 | all-reduce | flops 256 | bytes 2048 | tf_op jit(solution)/shard_map/psum | solution.py:180
  289.7 1.9 add_convert_fusion
  291.7 1.0 convert_element_type.151
  292.7 12.9 %all-to-all-start.1 = ((bf16[64,4,1024]{2,1,0:T(4,128)(2,1)}), bf16[64,4,1024]{2,1,0:T(4,128)(2,1)S(1)}, u32[]{:S(2)}, u32[]{:S(2)}) async-start(bf16[64,4,1024]{2,1,0:T(4,128)(2,1)} %convert_element_type.151), calls=%async_computation.2 | async-start | bytes 1048576 | tf_op jit(solution)/shard_map/all_to_all | solution.py:182
  306.3 16.9 %all-to-all-done.1 = bf16[64,4,1024]{2,1,0:T(4,128)(2,1)S(1)} async-done(((bf16[64,4,1024]{2,1,0:T(4,128)(2,1)}), bf16[64,4,1024]{2,1,0:T(4,128)(2,1)S(1)}, u32[]{:S(2)}, u32[]{:S(2)}) %all-to-all-start.1) | async-done | bytes 524320 | tf_op jit(solution)/shard_map/all_to_all | solution.py:182
  323.3 2.7 scatter_custom_fusion.6
  326.0 0.7 slice.42
  (148 shorter events, 11.4 us)
Async XLA Ops:
  7.2 92.7 %all-gather.3.cloned.1.call-start = ((), (), s32[]{:S(2)}) async-start(), calls=%async_computation.3 | async-start | bytes 8519680 | tf_op jit(solution)/shard_map/all_gather | solution.py:118
  22.9 15.9 %copy-start.39 = (bf16[1024]{0:T(1024)(128)(2,1)S(1)}, bf16[1024]{0:T(1024)(128)(2,1)}, u32[]{:S(2)}) copy-start(bf16[1024]{0:T(1024)(128)(2,1)} %param.12) | copy-start | bytes 6148
  24.4 33.8 %all-to-all-start = ((bf16[64,4,1024]{2,1,0:T(4,128)(2,1)}), bf16[64,4,1024]{2,1,0:T(4,128)(2,1)S(1)}, u32[]{:S(2)}, u32[]{:S(2)}) async-start(bf16[64,4,1024]{2,1,0:T(4,128)(2,1)} %select_select_fusion), calls=%async_computation | async-start | bytes 1048576 | tf_op jit(solution)/shard_map/all_to_all | solution.py:104
  38.8 97.4 %reduce-scatter.2.cloned.1.call-start = ((), (), s32[]{:S(2)}) async-start(), calls=%async_computation.4 | async-start | bytes 2621440 | tf_op jit(solution)/shard_map/reduce_scatter | solution.py:121
  64.9 35.0 %copy-start.31 = (f32[256]{0:T(256)}, f32[256]{0:T(256)S(1)}, u32[]{:S(2)}) copy-start(f32[256]{0:T(256)S(1)} %fusion.65) | copy-start | bytes 3076
  107.1 0.7 copy-start.26
  107.1 3.3 copy-start.41
  107.1 94.7 %all-reduce.5.cloned.1.call-start = ((), (), s32[]{:S(2)}) async-start(), calls=%async_computation.5 | async-start | bytes 131072 | tf_op jit(solution)/shard_map/psum | solution.py:142
  113.9 18.5 %copy-start.29 = (f32[256]{0:T(256)}, f32[256]{0:T(256)S(1)}, u32[]{:S(2)}) copy-start(f32[256]{0:T(256)S(1)} %gather_fusion.6) | copy-start | bytes 3076
  127.6 3.1 copy-start
  132.4 3.6 %copy-start.5 = (bf16[4,128,8,128]{1,3,2,0:T(8,128)(2,1)S(1)}, bf16[4,128,8,128]{1,3,2,0:T(8,128)(2,1)}, u32[]{:S(2)}) copy-start(bf16[4,128,8,128]{1,3,2,0:T(8,128)(2,1)} %copy.110) | copy-start | bytes 3145732
  142.1 2.4 copy-start.4
  146.5 2.9 copy-start.1
  146.5 2.9 copy-start.19
  146.5 3.5 %copy-start.6 = (bf16[4,128,8,128]{1,3,2,0:T(8,128)(2,1)S(1)}, bf16[4,128,8,128]{1,3,2,0:T(8,128)(2,1)}, u32[]{:S(2)}) copy-start(bf16[4,128,8,128]{1,3,2,0:T(8,128)(2,1)} %copy.110) | copy-start | bytes 3145732
  146.5 3.5 %copy-start.15 = (f32[4,128,8,128]{1,3,2,0:T(8,128)S(1)}, f32[4,128,8,128]{1,3,2,0:T(8,128)}, u32[]{:S(2)}) copy-start(f32[4,128,8,128]{1,3,2,0:T(8,128)} %copy.113) | copy-start | bytes 6291460
  149.4 1.5 copy-start.9
  158.0 108.7 %all-gather.5.cloned.1.call-start = ((), (), s32[]{:S(2)}) async-start(), calls=%async_computation.6 | async-start | bytes 2621440 | tf_op jit(solution)/shard_map/all_gather | solution.py:171
  166.7 37.5 %copy-start.27 = (bf16[4,128]{1,0:T(4,128)(2,1)}, bf16[4,128]{1,0:T(4,128)(2,1)S(1)}, u32[]{:S(2)}) copy-start(bf16[4,128]{1,0:T(4,128)(2,1)S(1)} %get-tuple-element.4) | copy-start | bytes 3076
  166.7 37.5 %copy-start.33 = (bf16[4,128]{1,0:T(4,128)(2,1)}, bf16[4,128]{1,0:T(4,128)(2,1)S(1)}, u32[]{:S(2)}) copy-start(bf16[4,128]{1,0:T(4,128)(2,1)S(1)} %get-tuple-element.5) | copy-start | bytes 3076
  204.1 1.7 copy-start.21
  204.2 0.8 copy-start.16
  204.2 1.6 copy-start.28
  204.2 1.6 copy-start.34
  204.2 1.6 copy-start.3
  204.2 1.6 copy-start.24
  209.3 2.3 copy-start.18
  211.6 3.3 copy-start.2
  211.6 3.3 copy-start.7
  211.6 3.8 %copy-start.10 = (f32[4,8,128,128]{2,3,1,0:T(8,128)S(1)}, f32[4,8,128,128]{2,3,1,0:T(8,128)}, u32[]{:S(2)}) copy-start(f32[4,8,128,128]{2,3,1,0:T(8,128)} %copy-done.9) | copy-start | bytes 6291460
  211.6 3.8 %copy-start.20 = (f32[4,128,8]{1,2,0:T(8,128)S(1)}, f32[4,128,8]{1,2,0:T(8,128)}, u32[]{:S(2)}) copy-start(f32[4,128,8]{1,2,0:T(8,128)} %copy-done.19) | copy-start | bytes 49156
  214.9 1.6 copy-start.17
  221.4 9.6 %copy-start.37 = (s32[4,64]{1,0:T(4,128)S(1)}, s32[4,64]{1,0:T(4,128)}, u32[]{:S(2)}) copy-start(s32[4,64]{1,0:T(4,128)} %get-tuple-element.17) | copy-start | bytes 3076
  221.4 9.7 %copy-start.35 = (s32[4,127]{1,0:T(4,128)S(1)}, s32[4,127]{1,0:T(4,128)}, u32[]{:S(2)}) copy-start(s32[4,127]{1,0:T(4,128)} %get-tuple-element.13) | copy-start | bytes 6100
  221.4 9.7 %copy-start.36 = (s32[4,1]{1,0:T(4,128)S(1)}, s32[4,1]{1,0:T(4,128)}, u32[]{:S(2)}) copy-start(s32[4,1]{1,0:T(4,128)} %get-tuple-element.15) | copy-start | bytes 52
  231.2 4.3 %copy-start.8 = (bf16[4,128,8,128]{1,3,2,0:T(8,128)(2,1)S(1)}, bf16[4,128,8,128]{1,3,2,0:T(8,128)(2,1)}, u32[]{:S(2)}) copy-start(bf16[4,128,8,128]{1,3,2,0:T(8,128)(2,1)} %copy.110) | copy-start | bytes 3145732
  231.2 4.3 %copy-start.11 = (f32[4,8,128,128]{2,3,1,0:T(8,128)S(1)}, f32[4,8,128,128]{2,3,1,0:T(8,128)}, u32[]{:S(2)}) copy-start(f32[4,8,128,128]{2,3,1,0:T(8,128)} %copy-done.9) | copy-start | bytes 6291460
  231.2 4.3 %copy-start.14 = (bf16[4,128,1024]{1,2,0:T(8,128)(2,1)S(1)}, bf16[4,128,1024]{1,2,0:T(8,128)(2,1)}, u32[]{:S(2)}) copy-start(bf16[4,128,1024]{1,2,0:T(8,128)(2,1)} %copy.130) | copy-start | bytes 3145732
  237.9 3.0 copy-start.38
  237.9 3.1 copy-start.30
  237.9 5.4 %copy-start.22 = (f32[4,128]{1,0:T(4,128)S(1)}, f32[4,128]{1,0:T(4,128)}, u32[]{:S(2)}) copy-start(f32[4,128]{1,0:T(4,128)} %copy-done.21) | copy-start | bytes 6148
  237.9 5.4 %copy-start.25 = (f32[4,128]{1,0:T(4,128)S(1)}, f32[4,128]{1,0:T(4,128)}, u32[]{:S(2)}) copy-start(f32[4,128]{1,0:T(4,128)} %get-tuple-element.23) | copy-start | bytes 6148
  261.0 13.1 %copy-start.12 = (f32[4,128,8,128]{3,2,1,0:T(8,128)S(1)}, f32[4,128,8,128]{3,2,1,0:T(8,128)}, u32[]{:S(2)}) copy-start(f32[4,128,8,128]{3,2,1,0:T(8,128)} %copy.123) | copy-start | bytes 6291460
  274.2 15.6 %copy-start.32 = (f32[256]{0:T(256)S(1)}, f32[256]{0:T(256)}, u32[]{:S(2)}) copy-start(f32[256]{0:T(256)} %copy-done.31) | copy-start | bytes 3076
  281.6 8.2 %copy-start.13 = (f32[256,1024]{1,0:T(8,128)S(1)}, f32[256,1024]{1,0:T(8,128)}, u32[]{:S(2)}) copy-start(f32[256,1024]{1,0:T(8,128)} %scatter_custom_fusion.1) | copy-start | bytes 3145732
  291.7 13.9 %copy-start.23 = (s32[1,64,4]{1,2,0:T(4,128)S(1)}, s32[1,64,4]{1,2,0:T(4,128)}, u32[]{:S(2)}) copy-start(s32[1,64,4]{1,2,0:T(4,128)} %param.9) | copy-start | bytes 3076
  291.7 14.1 %copy-start.40 = (f32[4]{0:T(128)S(1)}, f32[4]{0:T(128)}, u32[]{:S(2)}) copy-start(f32[4]{0:T(128)} %get-tuple-element.12) | copy-start | bytes 52
  291.7 14.1 %copy-start.42 = (s32[4]{0:T(128)S(1)}, s32[4]{0:T(128)}, u32[]{:S(2)}) copy-start(s32[4]{0:T(128)} %param.11) | copy-start | bytes 52
  292.7 30.5 %all-to-all-start.1 = ((bf16[64,4,1024]{2,1,0:T(4,128)(2,1)}), bf16[64,4,1024]{2,1,0:T(4,128)(2,1)S(1)}, u32[]{:S(2)}, u32[]{:S(2)}) async-start(bf16[64,4,1024]{2,1,0:T(4,128)(2,1)} %convert_element_type.151), calls=%async_computation.2 | async-start | bytes 1048576 | tf_op jit(solution)/shard_map/all_to_all | solution.py:182
Sparse Core Ops, SparseCore 0:
  10.7 89.1 all-gather.2
  107.3 28.5 reduce-scatter.1
  158.1 43.6 all-reduce.4
  231.1 35.5 all-gather.4
where the time goes:
time: 339 us; the launch traced here: 333 us
  waiting for transfers between devices  112 us (33%)
  other arithmetic  61.6 us (18%)
  local copies, waits for them, and re-layouts  50 us (15%)
  matrix products  37 us (11%)
  blocking collectives  30.5 us (9%)
  starting transfers between devices  27.5 us (8%)
  between operations  14.6 us (4%)
    all_gather x1, waiting for transfers between devices, local(): lax.all_gather(query_weight, 'sect', axis=1, tiled=True)  34.8 us
    psum x1, waiting for transfers between devices, local(): lax.psum(partial_stats[2].astype(jnp.bfloat16), 'tp').astype(jnp.float32)  34.6 us
    scatter-add x6, other arithmetic, segment_rows(): jax.ops.segment_sum(values.reshape((-1,) + values.shape[2:]), places.resh...  32.6 us
    all_to_all x1, waiting for transfers between devices, local(): lax.all_to_all(outgoing, 'sect', split_axis=0, concat_axis=0, tiled=True)  19.4 us
    all_to_all x1, waiting for transfers between devices, local(): lax.all_to_all(grad_slots.reshape(arrived.shape).astype(jnp.bfloat16), 's...  16.9 us
    all_to_all x1, starting transfers between devices, local(): lax.all_to_all(outgoing, 'sect', split_axis=0, concat_axis=0, tiled=True)  14.3 us
    all_to_all x1, starting transfers between devices, local(): lax.all_to_all(grad_slots.reshape(arrived.shape).astype(jnp.bfloat16), 's...  12.9 us
    unnamed x90, local copies, waits for them, and re-layouts  9.68 us
  transfers between devices with their start and end apart: 6, of which 5 were waited for; matrix products, arithmetic and copies ran while one was open for 20% of the time, Pallas kernels for 0%

commit v1 on v0

--- a/solution.py
+++ b/solution.py
@@ -115,7 +115,9 @@
     normed_low = normed_slots.astype(jnp.bfloat16)
     partial_query = jnp.dot(
         normed_low,
-        lax.all_gather(query_weight, "sect", axis=1, tiled=True),
+        jnp.concatenate(
+            lax.all_to_all(jnp.stack([query_weight] * lax.axis_size("sect")), "sect", 0, 0), axis=1
+        ),
         preferred_element_type=jnp.float32,
     )
     query_slots = lax.psum_scatter(

time: 339 us -> 500 us (1.47)
  waiting for transfers between devices: 112 us -> 243 us
  blocking collectives: 30.5 us -> 61.4 us
  starting transfers between devices: 27.5 us -> 19.2 us
    all_to_all x1, waiting for transfers between devices: 19.4 us -> 174 us  [local(): lax.all_to_all(jnp.stack([query_weight] * lax.axis_size('sect')), 'sect',...]
    all_gather x1, waiting for transfers between devices: 34.8 us -> 0.03 us  [local(): lax.all_gather(query_weight, 'sect', axis=1, tiled=True)]
    all_to_all x0 -> x1, blocking collectives: none -> 31.8 us  [local(): lax.all_to_all(outgoing, 'sect', split_axis=0, concat_axis=0, tiled=True)]
    reduce_scatter x1, waiting for transfers between devices: 0.02 us -> 10.3 us  [local(): lax.psum_scatter(partial_query.astype(jnp.bfloat16), 'tp', scatter_dimens...]
    all_to_all x1, starting transfers between devices: 14.3 us -> 6.01 us  [local(): lax.all_to_all(jnp.stack([query_weight] * lax.axis_size('sect')), 'sect',...]
    all_gather x1, waiting for transfers between devices: 5.71 us -> 12.2 us  [local(): lax.all_gather(grad_query_slots.astype(jnp.bfloat16), 'tp', axis=1, tiled...]
    psum x1, waiting for transfers between devices: 34.6 us -> 28.2 us  [local(): lax.psum(partial_stats[2].astype(jnp.bfloat16), 'tp').astype(jnp.float32)]
    unnamed x90 -> x84, local copies, waits for them, and re-layouts: 9.68 us -> 10.6 us
  transfers between devices with their start and end apart: 6 -> 6, of which waited for: 5 -> 5; matrix products, arithmetic and copies ran while one was open for 20% -> 18% of each run, Pallas kernels for 0% -> 0%
where the time goes in v1:
time: 500 us; the launch traced here: 493 us
  waiting for transfers between devices  243 us (49%)
  other arithmetic  61.9 us (12%)
  blocking collectives  61.4 us (12%)
  local copies, waits for them, and re-layouts  54.7 us (11%)
  matrix products  37.1 us (7%)
  starting transfers between devices  19.2 us (4%)
  between operations  16.3 us (3%)
    all_to_all x1, waiting for transfers between devices, local(): lax.all_to_all(jnp.stack([query_weight] * lax.axis_size('sect')), 'sect',...  174 us
    scatter-add x6, other arithmetic, segment_rows(): jax.ops.segment_sum(values.reshape((-1,) + values.shape[2:]), places.resh...  32.6 us
    all_to_all x1, blocking collectives, local(): lax.all_to_all(outgoing, 'sect', split_axis=0, concat_axis=0, tiled=True)  31.8 us
    psum x1, waiting for transfers between devices, local(): lax.psum(partial_stats[2].astype(jnp.bfloat16), 'tp').astype(jnp.float32)  28.2 us
    all_to_all x1, waiting for transfers between devices, local(): lax.all_to_all(grad_slots.reshape(arrived.shape).astype(jnp.bfloat16), 's...  16.9 us
    all_to_all x1, starting transfers between devices, local(): lax.all_to_all(grad_slots.reshape(arrived.shape).astype(jnp.bfloat16), 's...  12.8 us
    all_gather x1, waiting for transfers between devices, local(): lax.all_gather(grad_query_slots.astype(jnp.bfloat16), 'tp', axis=1, tiled...  12.2 us
    unnamed x84, local copies, waits for them, and re-layouts  10.6 us
  transfers between devices with their start and end apart: 6, of which 5 were waited for; matrix products, arithmetic and copies ran while one was open for 18% of the time, Pallas kernels for 0%

profile of v1, /device:TPU:1, one launch (start us, length us, event | category | flops | bytes accessed | tf_op | source)
XLA Modules:
  0.0 493.0 jit_solution(4477898634287077831)
XLA Ops:
  10.3 1.0 fusion.32
  11.3 9.3 %psum.42 = f32[64]{0:T(128)S(1)} all-reduce(f32[64]{0:T(128)S(1)} %fusion.32), channel_id=1, replica_groups=mesh['sect'=64,'tp'=4] {'tp'}, use_global_device_ids=true, to_apply=%region_1.0 | all-reduce | flops 64 | bytes 512 | tf_op jit(solution)/shard_map/psum | solution.py:96
  20.8 1.0 fusion.34
  21.9 1.2 gather_fusion
  23.7 31.8 %all_to_all.15 = bf16[64,4,1024]{2,1,0:T(4,128)(2,1)S(1)} all-to-all(bf16[64,4,1024]{2,1,0:T(4,128)(2,1)S(1)} %select_select_fusion), channel_id=1, replica_groups=mesh['sect'=64,'tp'=4] {'sect'}, dimensions={0} | all-to-all | bytes 1048576 | tf_op jit(solution)/shard_map/all_to_all | solution.py:104
  55.5 4.3 stack.2
  59.8 6.0 %all-to-all-start.1 = ((bf16[64,1024,64]{1,2,0:T(8,128)(2,1)}), bf16[64,1024,64]{1,2,0:T(8,128)(2,1)}, u32[]{:S(2)}, u32[]{:S(2)}) async-start(bf16[64,1024,64]{1,2,0:T(8,128)(2,1)} %stack.2), calls=%async_computation.1 | async-start | bytes 16777216 | tf_op jit(solution)/shard_map/all_to_all | solution.py:119
  66.3 6.8 %psum.43 = f32[256]{0:T(256)S(1)} all-reduce(f32[256]{0:T(256)S(1)} %reduce_sum.141), channel_id=1, replica_groups=mesh['sect'=64,'tp'=4] {'tp'}, use_global_device_ids=true, to_apply=%region_3.4 | all-reduce | flops 256 | bytes 2048 | tf_op jit(solution)/shard_map/psum | solution.py:108
  73.7 174.4 %all-to-all-done.1 = bf16[64,1024,64]{1,2,0:T(8,128)(2,1)} async-done(((bf16[64,1024,64]{1,2,0:T(8,128)(2,1)}), bf16[64,1024,64]{1,2,0:T(8,128)(2,1)}, u32[]{:S(2)}, u32[]{:S(2)}) %all-to-all-start.1) | async-done | bytes 8388640 | tf_op jit(solution)/shard_map/all_to_all | solution.py:119
  248.1 7.1 %convolution_convert_fusion = bf16[256,4096]{1,0:T(8,128)(2,1)} fusion(bf16[256,1024]{1,0:T(8,128)(2,1)S(1)} %convert_element_type.131, bf16[1024,4096]{0,1:T(8,128)(2,1)} %bitcast.7), kind=kOutput, calls=%fused_computation.14 | convolution fusion | flops 2148532224 | bytes 11010048 | tf_op jit(solution)/shard_map/dot_general | solution.py:116
  257.9 2.1 gather_fusion.2
  260.0 1.3 copy.132
  261.2 2.4 copy.111
  263.7 2.7 gather_fusion.1
  266.4 3.4 copy.134
  269.8 3.1 copy.114
  272.8 1.6 slice.40
  274.4 1.2 gather_fusion.5
  275.9 10.3 %reduce-scatter.2.cloned.1.call-done = bf16[256,1024]{1,0:T(8,128)(2,1)} async-done(((bf16[256,4096]{1,0:T(8,128)(2,1)}), bf16[256,1024]{1,0:T(8,128)(2,1)}) %reduce-scatter.2.cloned.1.call-update) | async-done | bytes 524304 | tf_op jit(solution)/shard_map/reduce_scatter | solution.py:123
  286.2 1.1 convert_element_type.133
  287.3 2.7 gather_fusion.3
  290.0 2.1 copy.133
  292.1 1.4 multiply_reduce_fusion.1
  293.5 1.0 copy.106
  294.5 1.9 copy.107
  296.5 2.8 fusion.20
  299.5 0.9 fusion.18
  300.8 1.8 copy.113
  302.6 3.2 multiply_reduce_fusion
  305.8 2.0 convolution_convert_fusion.5
  309.7 1.9 gather_fusion.6
  312.4 3.5 gather_fusion.4
  315.9 6.8 %all-reduce.2 = (bf16[4,128]{1,0:T(4,128)(2,1)S(1)}, bf16[4,128]{1,0:T(4,128)(2,1)S(1)}) all-reduce(bf16[4,128]{1,0:T(4,128)(2,1)S(1)} %get-tuple-element.27, bf16[4,128]{1,0:T(4,128)(2,1)S(1)} %get-tuple-element.10), channel_id=1, replica_groups=mesh['sect'=64,'tp'=4] {'tp'}, use_global_device_ids=true, to_apply=%region_11.12 | all-reduce | flops 1024 | bytes 4096 | tf_op jit(solution)/shard_map/psum | solution.py:142
  323.9 28.2 %all-reduce.5.cloned.1.call-done = bf16[4,128,64]{1,2,0:T(8,128)(2,1)} async-done(((bf16[4,128,64]{1,2,0:T(8,128)(2,1)}), bf16[4,128,64]{1,2,0:T(8,128)(2,1)}) %all-reduce.5.cloned.1.call-update) | async-done | bytes 65552 | tf_op jit(solution)/shard_map/psum | solution.py:144
  352.1 1.0 fusion.41
  353.0 1.3 fusion.67
  354.3 1.6 fusion.43
  356.2 1.3 copy-done.3
  357.6 3.5 pad_add_fusion
  361.1 2.3 copy.131
  363.4 3.3 fusion.5
  367.4 1.1 fusion.16
  368.5 1.9 add_add_fusion.1
  370.4 2.9 copy.121
  373.3 7.5 %scatter_custom_fusion.2 = f32[256,1024]{1,0:T(8,128)} fusion(s32[512]{0:T(512)} %get-tuple-element.20, f32[64,8,8,128]{3,2,1,0:T(8,128)} %bitcast.117, f32[]{:T(128)} %constant.17.clone.1), kind=kCustom, calls=%fused_computation.37 | custom fusion | flops 524288 | bytes 3146240 | tf_op jit(solution)/shard_map/scatter-add | solution.py:89
  380.8 2.1 convert_element_type.151
  383.1 4.4 fusion.9
  387.6 2.4 fusion.6
  390.0 3.0 copy.124
  393.1 2.3 scatter_custom_fusion.5
  395.4 2.3 fusion.46
  397.7 4.3 scatter_custom_fusion.1
  402.0 6.8 %scatter_custom_fusion = f32[256,1024]{1,0:T(8,128)} fusion(s32[512]{0:T(512)} %get-tuple-element.20, f32[512,1024]{1,0:T(8,128)} %bitcast.126, f32[]{:T(128)} %constant.17.clone.1), kind=kCustom, calls=%fused_computation.74 | custom fusion | flops 524288 | bytes 1049088 | tf_op jit(solution)/shard_map/scatter-add | solution.py:89
  408.8 4.2 scatter_custom_fusion.4
  413.1 12.2 %all-gather.3.cloned.1.call-done = bf16[256,4096]{1,0:T(8,128)(2,1)} async-done(((bf16[256,1024]{1,0:T(8,128)(2,1)}), bf16[256,4096]{1,0:T(8,128)(2,1)}) %all-gather.3.cloned.1.call-update) | async-done | bytes 2097168 | tf_op jit(solution)/shard_map/all_gather | solution.py:173
  425.3 7.4 %fusion.81 = f32[256,1024]{1,0:T(8,128)} fusion(bf16[256,4096]{1,0:T(8,128)(2,1)} %all-gather.3.cloned.1.call-done, bf16[1024,4096]{0,1:T(8,128)(2,1)} %all-gather.5.cloned.1.call-done), kind=kOutput, calls=%fused_computation.176 | convolution fusion | flops 2147483648 | bytes 11534336 | tf_op jit(solution)/shard_map/dot_general | solution.py:174
  432.7 7.4 %scatter_custom_fusion.3 = f32[256,1024]{1,0:T(8,128)} fusion(f32[256,1024]{1,0:T(8,128)} %fusion.81, s32[512]{0:T(512)} %get-tuple-element.20, f32[64,8,8,128]{3,2,1,0:T(8,128)S(1)} %bitcast.116), kind=kCustom, calls=%fused_computation.34 | custom fusion | flops 524288 | bytes 3145728 | tf_op jit(solution)/shard_map/scatter-add | solution.py:89
  440.1 1.5 multiply_reduce_fusion.2
  441.7 6.7 %psum.47 = f32[256]{0:T(256)S(1)} all-reduce(f32[256]{0:T(256)S(1)} %multiply_multiply_fusion.7), channel_id=1, replica_groups=mesh['sect'=64,'tp'=4] {'tp'}, use_global_device_ids=true, to_apply=%region_26.27 | all-reduce | flops 256 | bytes 2048 | tf_op jit(solution)/shard_map/psum | solution.py:182
  448.4 2.0 add_convert_fusion
  450.4 1.0 convert_element_type.159
  451.4 12.8 %all-to-all-start.2 = ((bf16[64,4,1024]{2,1,0:T(4,128)(2,1)}), bf16[64,4,1024]{2,1,0:T(4,128)(2,1)S(1)}, u32[]{:S(2)}, u32[]{:S(2)}) async-start(bf16[64,4,1024]{2,1,0:T(4,128)(2,1)} %convert_element_type.159), calls=%async_computation.3 | async-start | bytes 1048576 | tf_op jit(solution)/shard_map/all_to_all | solution.py:184
  465.0 16.9 %all-to-all-done.2 = bf16[64,4,1024]{2,1,0:T(4,128)(2,1)S(1)} async-done(((bf16[64,4,1024]{2,1,0:T(4,128)(2,1)}), bf16[64,4,1024]{2,1,0:T(4,128)(2,1)S(1)}, u32[]{:S(2)}, u32[]{:S(2)}) %all-to-all-start.2) | async-done | bytes 524320 | tf_op jit(solution)/shard_map/all_to_all | solution.py:184
  482.0 2.7 scatter_custom_fusion.6
  (147 shorter events, 14.3 us)
Async XLA Ops:
  23.0 32.5 %copy-start.18 = (bf16[1024,64]{0,1:T(8,128)(2,1)S(1)}, bf16[1024,64]{0,1:T(8,128)(2,1)}, u32[]{:S(2)}) copy-start(bf16[1024,64]{0,1:T(8,128)(2,1)} %param.13) | copy-start | bytes 393220
  59.8 6.1 %copy-start.36 = (bf16[1024]{0:T(1024)(128)(2,1)S(1)}, bf16[1024]{0:T(1024)(128)(2,1)}, u32[]{:S(2)}) copy-start(bf16[1024]{0:T(1024)(128)(2,1)} %param.12) | copy-start | bytes 6148
  59.8 188.3 %all-to-all-start.1 = ((bf16[64,1024,64]{1,2,0:T(8,128)(2,1)}), bf16[64,1024,64]{1,2,0:T(8,128)(2,1)}, u32[]{:S(2)}, u32[]{:S(2)}) async-start(bf16[64,1024,64]{1,2,0:T(8,128)(2,1)} %stack.2), calls=%async_computation.1 | async-start | bytes 16777216 | tf_op jit(solution)/shard_map/all_to_all | solution.py:119
  65.8 220.3 %reduce-scatter.2.cloned.1.call-start = ((), (), s32[]{:S(2)}) async-start(), calls=%async_computation.4 | async-start | bytes 2621440 | tf_op jit(solution)/shard_map/reduce_scatter | solution.py:123
  73.2 184.5 %copy-start.27 = (f32[256]{0:T(256)}, f32[256]{0:T(256)S(1)}, u32[]{:S(2)}) copy-start(f32[256]{0:T(256)S(1)} %fusion.68) | copy-start | bytes 3076
  255.3 0.7 copy-start.29
  255.3 2.0 copy-start.38
  255.3 96.8 %all-reduce.5.cloned.1.call-start = ((), (), s32[]{:S(2)}) async-start(), calls=%async_computation.5 | async-start | bytes 131072 | tf_op jit(solution)/shard_map/psum | solution.py:144
  269.8 3.1 copy-start
  274.4 1.2 copy-start.5
  292.1 2.4 copy-start.4
  296.5 2.9 copy-start.1
  296.5 2.9 copy-start.20
  296.5 2.9 copy-start.6
  296.5 3.0 copy-start.15
  299.4 1.4 copy-start.9
  307.8 105.3 %all-gather.5.cloned.1.call-start = ((), (), s32[]{:S(2)}) async-start(), calls=%async_computation.7 | async-start | bytes 8519680 | tf_op jit(solution)/shard_map/all_gather | solution.py:176
  308.4 116.9 %all-gather.3.cloned.1.call-start = ((), (), s32[]{:S(2)}) async-start(), calls=%async_computation.6 | async-start | bytes 2621440 | tf_op jit(solution)/shard_map/all_gather | solution.py:173
  311.7 0.6 copy-start.30
  354.3 1.9 copy-start.22
  356.0 1.6 copy-start.3
  356.0 1.6 copy-start.16
  356.0 1.6 copy-start.25
  361.1 2.3 copy-start.19
  363.4 3.3 copy-start.2
  363.4 3.3 copy-start.7
  363.4 4.0 copy-start.10
  363.4 4.0 copy-start.21
  366.7 1.8 copy-start.17
  373.3 9.7 %copy-start.34 = (s32[4,64]{1,0:T(4,128)S(1)}, s32[4,64]{1,0:T(4,128)}, u32[]{:S(2)}) copy-start(s32[4,64]{1,0:T(4,128)} %get-tuple-element.17) | copy-start | bytes 3076
  373.3 9.8 %copy-start.32 = (s32[4,127]{1,0:T(4,128)S(1)}, s32[4,127]{1,0:T(4,128)}, u32[]{:S(2)}) copy-start(s32[4,127]{1,0:T(4,128)} %get-tuple-element.13) | copy-start | bytes 6100
  373.3 9.8 %copy-start.33 = (s32[4,1]{1,0:T(4,128)S(1)}, s32[4,1]{1,0:T(4,128)}, u32[]{:S(2)}) copy-start(s32[4,1]{1,0:T(4,128)} %get-tuple-element.15) | copy-start | bytes 52
  383.1 4.5 copy-start.8
  383.1 4.5 copy-start.11
  383.1 4.5 copy-start.14
  390.0 3.0 copy-start.35
  390.0 3.1 copy-start.31
  390.0 5.4 %copy-start.23 = (f32[4,128]{1,0:T(4,128)S(1)}, f32[4,128]{1,0:T(4,128)}, u32[]{:S(2)}) copy-start(f32[4,128]{1,0:T(4,128)} %copy-done.22) | copy-start | bytes 6148
  390.0 5.4 %copy-start.26 = (f32[4,128]{1,0:T(4,128)S(1)}, f32[4,128]{1,0:T(4,128)}, u32[]{:S(2)}) copy-start(f32[4,128]{1,0:T(4,128)} %get-tuple-element.23) | copy-start | bytes 6148
  413.1 19.6 %copy-start.12 = (f32[4,128,8,128]{3,2,1,0:T(8,128)S(1)}, f32[4,128,8,128]{3,2,1,0:T(8,128)}, u32[]{:S(2)}) copy-start(f32[4,128,8,128]{3,2,1,0:T(8,128)} %copy.124) | copy-start | bytes 6291460
  432.7 15.6 %copy-start.28 = (f32[256]{0:T(256)S(1)}, f32[256]{0:T(256)}, u32[]{:S(2)}) copy-start(f32[256]{0:T(256)} %copy-done.27) | copy-start | bytes 3076
  440.1 8.2 %copy-start.13 = (f32[256,1024]{1,0:T(8,128)S(1)}, f32[256,1024]{1,0:T(8,128)}, u32[]{:S(2)}) copy-start(f32[256,1024]{1,0:T(8,128)} %scatter_custom_fusion.1) | copy-start | bytes 3145732
  450.3 13.9 %copy-start.24 = (s32[1,64,4]{1,2,0:T(4,128)S(1)}, s32[1,64,4]{1,2,0:T(4,128)}, u32[]{:S(2)}) copy-start(s32[1,64,4]{1,2,0:T(4,128)} %param.9) | copy-start | bytes 3076
  450.3 14.1 %copy-start.37 = (f32[4]{0:T(128)S(1)}, f32[4]{0:T(128)}, u32[]{:S(2)}) copy-start(f32[4]{0:T(128)} %get-tuple-element.12) | copy-start | bytes 52
  450.4 14.1 %copy-start.39 = (s32[4]{0:T(128)S(1)}, s32[4]{0:T(128)}, u32[]{:S(2)}) copy-start(s32[4]{0:T(128)} %param.11) | copy-start | bytes 52
  451.4 30.5 %all-to-all-start.2 = ((bf16[64,4,1024]{2,1,0:T(4,128)(2,1)}), bf16[64,4,1024]{2,1,0:T(4,128)(2,1)S(1)}, u32[]{:S(2)}, u32[]{:S(2)}) async-start(bf16[64,4,1024]{2,1,0:T(4,128)(2,1)} %convert_element_type.159), calls=%async_computation.3 | async-start | bytes 1048576 | tf_op jit(solution)/shard_map/all_to_all | solution.py:184
Sparse Core Ops, SparseCore 0:
  255.4 30.7 reduce-scatter.1
  307.9 44.0 all-reduce.4
Sparse Core Ops, SparseCore 1:
  311.0 83.3 all-gather.4
  396.0 29.2 all-gather.2
